TPU v7x, 512 devices: a whole 4x4x16 slice. The times are simulated.
512 devices in a mesh: section: 16 (over y_hi, x, core), expert: 32 (over z, y_lo).
Axes of the slice: x: 4, y: 4 (y_hi: 2, y_lo: 2; y = y_hi * 2 + y_lo), z: 16, core: 2. Of those that a mesh axis runs over, the one named last changes fastest.
Arguments:
- ahead_rows: bfloat16 [16, 384, 7168], P('section', None, 'expert'), may hold values from -6 to 6
- behind_rows: bfloat16 [16, 384, 7168], P('section', None, 'expert'), may hold values from -6 to 6
- behind_grad: bfloat16 [16, 384, 7168], P('section', None, 'expert'), may hold values from -6 to 6
- route_scores: float32 [16, 2, 384], P('section'), may hold values from 0.1 to 1
- route_counts: int32 [16, 2], P('section'), may hold values from 96 to 384, as said below
- gate_up: bfloat16 [16, 32, 2, 256, 1792], P('section', 'expert'), may hold values from -0.0625 to 0.0625
- down_proj: bfloat16 [16, 32, 256, 1792], P('section', 'expert'), may hold values from -0.125 to 0.125
Outputs:
- ahead_sent: bfloat16 [16, 384, 7168], P('section', None, 'expert')
- behind_sent: bfloat16 [16, 384, 7168], P('section', None, 'expert')
Inputs may be any that keep to these rules, and one draw needn't show every extreme that they name: `route_counts`: live slots of each section's expert per micro-batch; in each micro-batch some section has all 384 slots live.
All inputs are finite; a program needn't handle non-finite values.
Results may differ from a plain program's by a relative error of at most 0.02.
Values may be sent and summed in bfloat16 or wider, within the bound.
A program may use at most 64 MiB of HBM per device.

v0:
```python
import jax
import jax.numpy as jnp
from jax import lax
from jax.sharding import PartitionSpec as P

DBLOCKS = 4


def partner_2(value, axis, stride):
    mask = 2**stride
    pairs = [(source, source ^ mask) for source in range(lax.axis_size(axis))]
    return lax.ppermute(value, axis, pairs)


def from_behind(shard, axis, by):
    devices = lax.axis_size(axis)
    pairs = [(i, i + by) for i in range(devices) if 0 <= i + by < devices]
    return lax.ppermute(shard, axis, pairs)


def silu_float(value):
    return value * jax.nn.sigmoid(value)


def upper_side(own_index, bit_level):
    return own_index >> bit_level & 1 == 1


def activate(partials, units):
    pre_ahead = partials[:, : 2 * units]
    gate_val = partials[:, 2 * units : 3 * units]
    up_val = partials[:, 3 * units : 4 * units]
    expanded = partials[:, 4 * units :]
    hidden = (silu_float(pre_ahead[:, :units]) * pre_ahead[:, units:]).astype(jnp.bfloat16)
    sigmoid_gate = jax.nn.sigmoid(gate_val)
    grad_gate = (expanded * up_val * sigmoid_gate * (1.0 + gate_val * (1.0 - sigmoid_gate))).astype(
        jnp.bfloat16
    )
    grad_up = (expanded * gate_val * sigmoid_gate).astype(jnp.bfloat16)
    return (hidden, grad_gate, grad_up)


def body(ahead_rows, behind_rows, behind_grad, route_scores, route_counts, gate_up, down_proj):
    groups = lax.axis_size("expert")
    fgroups = groups // DBLOCKS
    low_bits = fgroups.bit_length() - 1
    height = ahead_rows.shape[1]
    own_index = lax.axis_index("expert")
    weights_in = gate_up[0, 0]
    weights_out = down_proj[0, 0]
    units = weights_in.shape[1]
    slot_ids = jnp.arange(height, dtype=jnp.int32)
    scale_ahead = route_scores[0, 0] * (slot_ids < route_counts[0, 0]).astype(jnp.float32)
    scale_behind = route_scores[0, 1] * (slot_ids < route_counts[0, 1]).astype(jnp.float32)
    scaled_grad = (behind_grad[0].astype(jnp.float32) * scale_behind[:, None]).astype(jnp.bfloat16)
    block_rows = jnp.stack([ahead_rows[0], behind_rows[0], scaled_grad])
    for bit_level in range(low_bits):
        partner = partner_2(block_rows, "expert", bit_level)
        block_rows = jnp.where(
            upper_side(own_index, bit_level),
            jnp.concatenate([partner, block_rows], axis=2),
            jnp.concatenate([block_rows, partner], axis=2),
        )
    pre_both = jnp.einsum(
        "mcd,kfd->mckf", block_rows[:2], weights_in, preferred_element_type=jnp.float32
    )
    expanded = lax.dot_general(
        block_rows[2], weights_out, (((1,), (1,)), ((), ())), preferred_element_type=jnp.float32
    )
    partials = jnp.concatenate(
        [pre_both[0].reshape(height, 2 * units), pre_both[1].reshape(height, 2 * units), expanded],
        axis=1,
    )
    for bit_level in (low_bits, low_bits + 1):
        partials = partials + partner_2(partials.astype(jnp.bfloat16), "expert", bit_level).astype(
            partials.dtype
        )
    hidden, grad_gate, grad_up = activate(partials, units)
    part_ahead = jnp.dot(hidden, weights_out, preferred_element_type=jnp.float32)
    grads_stacked = jnp.stack([grad_gate, grad_up], axis=1)
    part_behind = jnp.einsum(
        "ckf,kfd->cd", grads_stacked, weights_in, preferred_element_type=jnp.float32
    )
    outputs = jnp.stack([part_ahead, part_behind])
    for bit_level in reversed(range(low_bits)):
        half = outputs.shape[2] // 2
        upper_half = upper_side(own_index, bit_level)
        keep_part = jnp.where(upper_half, outputs[:, :, half:], outputs[:, :, :half])
        send_part = jnp.where(upper_half, outputs[:, :, :half], outputs[:, :, half:])
        outputs = keep_part + partner_2(send_part.astype(jnp.bfloat16), "expert", bit_level).astype(
            send_part.dtype
        )
    ahead_out = (outputs[0] * scale_ahead[:, None]).astype(jnp.bfloat16)
    behind_out = outputs[1].astype(jnp.bfloat16)
    moved_ahead = from_behind(ahead_out, "section", 1)
    moved_behind = from_behind(behind_out, "section", -1)
    return (moved_ahead[None], moved_behind[None])


def solution(mesh):
    in_specs = (
        P("section", None, "expert"),
        P("section", None, "expert"),
        P("section", None, "expert"),
        P("section", None, None),
        P("section", None),
        P("section", "expert", None, None, None),
        P("section", "expert", None, None),
    )
    out_specs = (P("section", None, "expert"), P("section", None, "expert"))
    return jax.shard_map(body, mesh=mesh, in_specs=in_specs, out_specs=out_specs, check_vma=False)
```

profile of v0, /device:TPU:88, one launch (start us, length us, event | category | flops | bytes accessed | tf_op | source)
XLA Modules:
  0.0 467.8 jit_solution(16671511683652418589)
XLA Ops:
  6.0 2.7 collective-permute-start
  8.7 12.7 %collective-permute-done = bf16[3,384,224]{1,2,0:T(8,128)(2,1)S(1)} collective-permute-done((bf16[3,384,224]{1,2,0:T(8,128)(2,1)S(1)}, bf16[3,384,224]{1,2,0:T(8,128)(2,1)S(1)}, u32[]{:S(2)}, u32[]{:S(2)}) %collective-permute-start) | collective-permute-done | bytes 516128 | tf_op jit(solution)/shard_map/ppermute | solution.py:12
  21.4 1.5 maximum_select_fusion.2
  22.8 3.8 collective-permute-start.1
  26.7 22.0 %collective-permute-done.1 = bf16[3,384,448]{1,2,0:T(8,128)(2,1)} collective-permute-done((bf16[3,384,448]{1,2,0:T(8,128)(2,1)S(1)}, bf16[3,384,448]{1,2,0:T(8,128)(2,1)}, u32[]{:S(2)}, u32[]{:S(2)}) %collective-permute-start.1) | collective-permute-done | bytes 1032224 | tf_op jit(solution)/shard_map/ppermute | solution.py:12
  48.7 3.4 maximum_select_fusion.1
  52.1 1.9 collective-permute-start.2
  54.0 87.4 %collective-permute-done.2 = bf16[3,384,896]{1,2,0:T(8,128)(2,1)} collective-permute-done((bf16[3,384,896]{1,2,0:T(8,128)(2,1)}, bf16[3,384,896]{1,2,0:T(8,128)(2,1)}, u32[]{:S(2)}, u32[]{:S(2)}) %collective-permute-start.2) | collective-permute-done | bytes 2064416 | tf_op jit(solution)/shard_map/ppermute | solution.py:12
  141.4 4.9 %maximum_select_fusion = bf16[3,384,1792]{1,2,0:T(8,128)(2,1)S(1)} fusion(bf16[3,384,896]{1,2,0:T(8,128)(2,1)} %maximum_select_fusion.1, bf16[3,384,896]{1,2,0:T(8,128)(2,1)} %collective-permute-done.2, pred[]{:T(512)S(6)} %eq.14), kind=kLoop, calls=%fused_computation.2 | loop fusion | flops 18579456 | bytes 8257537 | tf_op jit(solution)/shard_map/jit(_where)/select_n | solution.py:59
  147.6 1.6 fusion.1
  150.6 1.4 copy.35
  153.1 9.1 %collective-permute-start.3 = (bf16[384,1280]{1,0:T(8,128)(2,1)S(1)}, bf16[384,1280]{1,0:T(8,128)(2,1)S(1)}, u32[]{:S(2)}, u32[]{:S(2)}) collective-permute-start(bf16[384,1280]{1,0:T(8,128)(2,1)S(1)} %fusion.4), channel_id=1, source_target_pairs={{0,8},{1,9},{2,10},{3,11},{4,12},{5,13},{6,14},{7,15},{8,0},{9,1},... | collective-permute-start | bytes 2949128 | tf_op jit(solution)/shard_map/ppermute | solution.py:12
  162.2 62.3 %collective-permute-done.3 = bf16[384,1280]{1,0:T(8,128)(2,1)S(1)} collective-permute-done((bf16[384,1280]{1,0:T(8,128)(2,1)S(1)}, bf16[384,1280]{1,0:T(8,128)(2,1)S(1)}, u32[]{:S(2)}, u32[]{:S(2)}) %collective-permute-start.3) | collective-permute-done | bytes 983072 | tf_op jit(solution)/shard_map/ppermute | solution.py:12
  224.8 10.5 %collective-permute-start.4 = (bf16[384,1280]{1,0:T(8,128)(2,1)S(1)}, bf16[384,1280]{1,0:T(8,128)(2,1)S(1)}, u32[]{:S(2)}, u32[]{:S(2)}) collective-permute-start(bf16[384,1280]{1,0:T(8,128)(2,1)S(1)} %fusion.8), channel_id=1, source_target_pairs={{0,16},{1,17},{2,18},{3,19},{4,20},{5,21},{6,22},{7,23},{8,24},{9,... | collective-permute-start | bytes 2949128 | tf_op jit(solution)/shard_map/ppermute | solution.py:12
  235.2 22.1 %collective-permute-done.4 = bf16[384,1280]{1,0:T(8,128)(2,1)S(1)} collective-permute-done((bf16[384,1280]{1,0:T(8,128)(2,1)S(1)}, bf16[384,1280]{1,0:T(8,128)(2,1)S(1)}, u32[]{:S(2)}, u32[]{:S(2)}) %collective-permute-start.4) | collective-permute-done | bytes 983072 | tf_op jit(solution)/shard_map/ppermute | solution.py:12
  261.1 113.5 %collective-permute-start.5 = (bf16[2,384,896]{1,2,0:T(8,128)(2,1)S(1)}, bf16[2,384,896]{1,2,0:T(8,128)(2,1)S(1)}, u32[]{:S(2)}, u32[]{:S(2)}) collective-permute-start(bf16[2,384,896]{1,2,0:T(8,128)(2,1)S(1)} %select_convert_fusion), channel_id=1, source_target_pairs={{0,4},{1,5},{2,6},{3,7},{4,0},{5,1},{6,2},{7,3},{8,12},{9,13},{10,... | collective-permute-start | bytes 4128776 | tf_op jit(solution)/shard_map/ppermute | solution.py:12
  374.5 31.8 %collective-permute-done.5 = bf16[2,384,896]{1,2,0:T(8,128)(2,1)S(1)} collective-permute-done((bf16[2,384,896]{1,2,0:T(8,128)(2,1)S(1)}, bf16[2,384,896]{1,2,0:T(8,128)(2,1)S(1)}, u32[]{:S(2)}, u32[]{:S(2)}) %collective-permute-start.5) | collective-permute-done | bytes 1376288 | tf_op jit(solution)/shard_map/ppermute | solution.py:12
  406.9 18.3 %collective-permute-start.6 = (bf16[2,384,448]{1,2,0:T(8,128)(2,1)S(1)}, bf16[2,384,448]{1,2,0:T(8,128)(2,1)S(1)}, u32[]{:S(2)}, u32[]{:S(2)}) collective-permute-start(bf16[2,384,448]{1,2,0:T(8,128)(2,1)S(1)} %select_convert_fusion.1), channel_id=1, source_target_pairs={{0,2},{1,3},{2,0},{3,1},{4,6},{5,7},{6,4},{7,5},{8,10},{9,11},{10,... | collective-permute-start | bytes 2064392 | tf_op jit(solution)/shard_map/ppermute | solution.py:12
  425.2 15.6 %collective-permute-done.6 = bf16[2,384,448]{1,2,0:T(8,128)(2,1)S(1)} collective-permute-done((bf16[2,384,448]{1,2,0:T(8,128)(2,1)S(1)}, bf16[2,384,448]{1,2,0:T(8,128)(2,1)S(1)}, u32[]{:S(2)}, u32[]{:S(2)}) %collective-permute-start.6) | collective-permute-done | bytes 688160 | tf_op jit(solution)/shard_map/ppermute | solution.py:12
  441.1 2.7 collective-permute-start.7
  444.4 8.0 %collective-permute-done.7 = bf16[2,384,224]{1,2,0:T(8,128)(2,1)S(1)} collective-permute-done((bf16[2,384,224]{1,2,0:T(8,128)(2,1)S(1)}, bf16[2,384,224]{1,2,0:T(8,128)(2,1)S(1)}, u32[]{:S(2)}, u32[]{:S(2)}) %collective-permute-start.7) | collective-permute-done | bytes 344096 | tf_op jit(solution)/shard_map/ppermute | solution.py:12
  452.6 3.5 collective-permute-start.9
  456.1 1.9 collective-permute-start.8
  459.0 7.5 %collective-permute-done.8 = bf16[384,224]{0,1:T(8,128)(2,1)S(1)} collective-permute-done((bf16[384,224]{0,1:T(8,128)(2,1)S(1)}, bf16[384,224]{0,1:T(8,128)(2,1)S(1)}, u32[]{:S(2)}, u32[]{:S(2)}) %collective-permute-start.8) | collective-permute-done | bytes 172064 | tf_op jit(solution)/shard_map/ppermute | solution.py:18
  (36 shorter events, 16.8 us)
Async XLA Ops:
  0.6 147.0 %copy-start = (bf16[1,1,2,256,1792]{4,3,2,1,0:T(8,128)(2,1)S(1)}, bf16[1,1,2,256,1792]{4,3,2,1,0:T(8,128)(2,1)}, u32[]{:S(2)}) copy-start(bf16[1,1,2,256,1792]{4,3,2,1,0:T(8,128)(2,1)} %param.12) | copy-start | bytes 5505028
  6.0 15.4 %collective-permute-start = (bf16[3,384,224]{1,2,0:T(8,128)(2,1)S(1)}, bf16[3,384,224]{1,2,0:T(8,128)(2,1)S(1)}, u32[]{:S(2)}, u32[]{:S(2)}) collective-permute-start(bf16[3,384,224]{1,2,0:T(8,128)(2,1)S(1)} %pad_maximum_fusion.2), channel_id=1, source_target_pairs={{0,1},{1,0},{2,3},{3,2},{4,5},{5,4},{6,7},{7,6},{8,9},{9,8},{10,11... | collective-permute-start | bytes 1548296 | tf_op jit(solution)/shard_map/ppermute | solution.py:12
  22.8 25.9 %collective-permute-start.1 = (bf16[3,384,448]{1,2,0:T(8,128)(2,1)S(1)}, bf16[3,384,448]{1,2,0:T(8,128)(2,1)}, u32[]{:S(2)}, u32[]{:S(2)}) collective-permute-start(bf16[3,384,448]{1,2,0:T(8,128)(2,1)S(1)} %maximum_select_fusion.2), channel_id=1, source_target_pairs={{0,2},{1,3},{2,0},{3,1},{4,6},{5,7},{6,4},{7,5},{8,10},{9,11},{10,... | collective-permute-start | bytes 3096584 | tf_op jit(solution)/shard_map/ppermute | solution.py:12
  52.1 89.3 %collective-permute-start.2 = (bf16[3,384,896]{1,2,0:T(8,128)(2,1)}, bf16[3,384,896]{1,2,0:T(8,128)(2,1)}, u32[]{:S(2)}, u32[]{:S(2)}) collective-permute-start(bf16[3,384,896]{1,2,0:T(8,128)(2,1)} %maximum_select_fusion.1), channel_id=1, source_target_pairs={{0,4},{1,5},{2,6},{3,7},{4,0},{5,1},{6,2},{7,3},{8,12},{9,13},{10,... | collective-permute-start | bytes 6193160 | tf_op jit(solution)/shard_map/ppermute | solution.py:12
  54.0 92.3 %copy-start.2 = (bf16[1,1,256,1792]{3,2,1,0:T(8,128)(2,1)S(1)}, bf16[1,1,256,1792]{3,2,1,0:T(8,128)(2,1)}, u32[]{:S(2)}) copy-start(bf16[1,1,256,1792]{3,2,1,0:T(8,128)(2,1)} %param.13) | copy-start | bytes 2752516
  152.0 72.6 %copy-start.1 = (f32[384,256]{1,0:T(8,128)S(1)}, f32[384,256]{1,0:T(8,128)}, u32[]{:S(2)}) copy-start(f32[384,256]{1,0:T(8,128)} %fusion.5) | copy-start | bytes 1179652
  153.1 71.4 %collective-permute-start.3 = (bf16[384,1280]{1,0:T(8,128)(2,1)S(1)}, bf16[384,1280]{1,0:T(8,128)(2,1)S(1)}, u32[]{:S(2)}, u32[]{:S(2)}) collective-permute-start(bf16[384,1280]{1,0:T(8,128)(2,1)S(1)} %fusion.4), channel_id=1, source_target_pairs={{0,8},{1,9},{2,10},{3,11},{4,12},{5,13},{6,14},{7,15},{8,0},{9,1},... | collective-permute-start | bytes 2949128 | tf_op jit(solution)/shard_map/ppermute | solution.py:12
  224.8 32.6 %collective-permute-start.4 = (bf16[384,1280]{1,0:T(8,128)(2,1)S(1)}, bf16[384,1280]{1,0:T(8,128)(2,1)S(1)}, u32[]{:S(2)}, u32[]{:S(2)}) collective-permute-start(bf16[384,1280]{1,0:T(8,128)(2,1)S(1)} %fusion.8), channel_id=1, source_target_pairs={{0,16},{1,17},{2,18},{3,19},{4,20},{5,21},{6,22},{7,23},{8,24},{9,... | collective-permute-start | bytes 2949128 | tf_op jit(solution)/shard_map/ppermute | solution.py:12
  257.7 1.2 copy-start.3
  261.1 145.3 %collective-permute-start.5 = (bf16[2,384,896]{1,2,0:T(8,128)(2,1)S(1)}, bf16[2,384,896]{1,2,0:T(8,128)(2,1)S(1)}, u32[]{:S(2)}, u32[]{:S(2)}) collective-permute-start(bf16[2,384,896]{1,2,0:T(8,128)(2,1)S(1)} %select_convert_fusion), channel_id=1, source_target_pairs={{0,4},{1,5},{2,6},{3,7},{4,0},{5,1},{6,2},{7,3},{8,12},{9,13},{10,... | collective-permute-start | bytes 4128776 | tf_op jit(solution)/shard_map/ppermute | solution.py:12
  406.8 36.9 %copy-start.4 = (f32[384]{0:T(512)S(1)}, f32[384]{0:T(512)}, u32[]{:S(2)}) copy-start(f32[384]{0:T(512)} %get-tuple-element.6) | copy-start | bytes 4612
  406.9 33.9 %collective-permute-start.6 = (bf16[2,384,448]{1,2,0:T(8,128)(2,1)S(1)}, bf16[2,384,448]{1,2,0:T(8,128)(2,1)S(1)}, u32[]{:S(2)}, u32[]{:S(2)}) collective-permute-start(bf16[2,384,448]{1,2,0:T(8,128)(2,1)S(1)} %select_convert_fusion.1), channel_id=1, source_target_pairs={{0,2},{1,3},{2,0},{3,1},{4,6},{5,7},{6,4},{7,5},{8,10},{9,11},{10,... | collective-permute-start | bytes 2064392 | tf_op jit(solution)/shard_map/ppermute | solution.py:12
  441.1 11.3 %collective-permute-start.7 = (bf16[2,384,224]{1,2,0:T(8,128)(2,1)S(1)}, bf16[2,384,224]{1,2,0:T(8,128)(2,1)S(1)}, u32[]{:S(2)}, u32[]{:S(2)}) collective-permute-start(bf16[2,384,224]{1,2,0:T(8,128)(2,1)S(1)} %select_convert_fusion.2), channel_id=1, source_target_pairs={{0,1},{1,0},{2,3},{3,2},{4,5},{5,4},{6,7},{7,6},{8,9},{9,8},{10,11... | collective-permute-start | bytes 1032200 | tf_op jit(solution)/shard_map/ppermute | solution.py:12
  452.6 6.4 %collective-permute-start.9 = (bf16[384,224]{0,1:T(8,128)(2,1)S(1)}, bf16[384,224]{0,1:T(8,128)(2,1)S(1)}, u32[]{:S(2)}, u32[]{:S(2)}) collective-permute-start(bf16[384,224]{0,1:T(8,128)(2,1)S(1)} %fusion.22), channel_id=1, source_target_pairs={{32,0},{64,32},{96,64},{128,96},{160,128},{192,160},{224,192},{256... | collective-permute-start | bytes 516104 | tf_op jit(solution)/shard_map/ppermute | solution.py:18
  456.1 10.3 %collective-permute-start.8 = (bf16[384,224]{0,1:T(8,128)(2,1)S(1)}, bf16[384,224]{0,1:T(8,128)(2,1)S(1)}, u32[]{:S(2)}, u32[]{:S(2)}) collective-permute-start(bf16[384,224]{0,1:T(8,128)(2,1)S(1)} %fusion.17), channel_id=1, source_target_pairs={{0,32},{32,64},{64,96},{96,128},{128,160},{160,192},{192,224},{224... | collective-permute-start | bytes 516104 | tf_op jit(solution)/shard_map/ppermute | solution.py:18
where the time goes:
time: 468 us
  waiting for transfers between devices  270 us (58%)
  starting transfers between devices  168 us (36%)
  other arithmetic  16.1 us (3%)
  local copies, waits for them, and re-layouts  7.77 us (2%)
  matrix products  4.85 us (1%)
    ppermute x8, waiting for transfers between devices, partner_2(): return lax.ppermute(value, axis, pairs)  262 us
    ppermute x8, starting transfers between devices, partner_2(): return lax.ppermute(value, axis, pairs)  162 us
    select_n x3, other arithmetic, body(): jnp.where(upper_side(own_index, bit_level), jnp.concatenate([partner, blo...  9.76 us
  transfers between devices with their start and end apart: 10, of which 10 were waited for; matrix products, arithmetic and copies ran while one was open for 0% of the time, Pallas kernels for 0%

commit v1 on v0

v1 whole, which is shorter than its diff:
```python
import functools

import jax
import jax.numpy as jnp
from jax import lax
from jax.experimental import pallas as pl
from jax.experimental.pallas import tpu as pltpu
from jax.sharding import PartitionSpec as P

MESH = pl.DeviceIdType.MESH
DBLOCKS = 4
LINE = 4
CHUNK = 128
F32 = jnp.float32
BF16 = jnp.bfloat16


def layer_kernel(
    chunks, sections, xin, gate_up, down, scale, out_ref,
    xall, wt, pf, pb, rs_in, rl_out, actb, oacc, obf, y_in, zl_send, zr_send, zl_in, zr_in, fin, landed, fsum,
    ag_send, ag_recv, rs_send, rs_recv, aq_send, aq_recv, y_send, y_recv, z_send, z_recv, s_send, s_recv,
):
    feats = xin.shape[1]
    units = down.shape[0]
    half = units // (2 * DBLOCKS)
    me = lax.axis_index("expert")
    sec = lax.axis_index("section")
    devices = lax.axis_size("expert")
    col = me % 2
    z = me // 2
    line = z % LINE
    q = z // LINE
    q_up, q_down = (q + 1) % DBLOCKS, (q + 3) % DBLOCKS

    def expert(index):
        return {"expert": index % devices}

    right, left = expert(me + 2), expert(me + devices - 2)
    across = {"expert": z * 2 + (1 - col)}
    ahead_q, back_q = expert(me + 2 * LINE), expert(me + devices - 2 * LINE)
    sec_up = {"section": (sec + 1) % sections}
    sec_down = {"section": (sec + sections - 1) % sections}

    barrier = pltpu.get_barrier_semaphore()
    for peer in (right, left, across, ahead_q, back_q, sec_up, sec_down):
        pl.semaphore_signal(barrier, inc=1, device_id=peer, device_id_type=MESH)
    pl.semaphore_wait(barrier, 7)

    drains = []

    def remote(src, dst, send, recv, device):
        return pltpu.make_async_remote_copy(
            src_ref=src, dst_ref=dst, send_sem=send, recv_sem=recv, device_id=device, device_id_type=MESH
        )

    def post(copy, cond=None):
        if cond is None:
            copy.start()
        else:
            pl.when(cond)(lambda: copy.start())
        drains.append((copy, cond))

    def arrived(ref, recv):
        remote(ref, ref, recv, recv, across).wait_recv()

    def rows_of(position, column):
        return pl.ds(pl.multiple_of((position * 2 + column) * feats, 16), feats)

    def slot_of(position, column):
        return position * 2 + column

    def gather_own(j):
        spot = xall.at[j, rows_of(line, col), :]
        sem = ag_recv.at[j, slot_of(line, col)]
        post(remote(xin.at[j], spot, ag_send.at[j, 0], sem, right), line < LINE - 1)
        post(remote(xin.at[j], spot, ag_send.at[j, 1], sem, left), line > 0)
        post(remote(xin.at[j], spot, ag_send.at[j, 2], sem, across))
        xall[j, rows_of(line, col), :] = xin[j]

    def gather_step(j, t):
        for side in (0, 1):
            there = line >= t if side == 0 else line + t < LINE
            source = (line - t) & 3 if side == 0 else (line + t) & 3
            spot = xall.at[j, rows_of(source, col), :]
            sem = ag_recv.at[j, slot_of(source, col)]
            pl.when(there)(functools.partial(arrived, spot, sem))
            if t < LINE - 1:
                onward = jnp.logical_and(there, line < LINE - 1 if side == 0 else line > 0)
                post(remote(spot, spot, ag_send.at[j, 3 * t + side], sem, right if side == 0 else left), onward)
            post(remote(spot, spot, ag_send.at[j, 12 + 2 * t + side], sem, across), there)

    def gather_rest(j):
        for position in range(LINE):
            arrived(xall.at[j, rows_of(position, 1 - col), :], ag_recv.at[j, slot_of(position, 1 - col)])

    def first_matmul(j):
        def keep(value, comp):
            for block in range(DBLOCKS):
                for part in range(2):
                    rows = value[(2 * block + part) * half : (2 * block + part + 1) * half]
                    pf[j, block, part, comp] = rows
                    pb[j, block, part, comp] = rows.astype(BF16)

        for k in range(2):
            value = jnp.dot(gate_up[k], xall[j, :, : 2 * CHUNK], preferred_element_type=F32)
            keep(value[:, :CHUNK], k)
            keep(value[:, CHUNK:], 2 + k)
        keep(jnp.dot(down[...], xall[j, :, 2 * CHUNK :], preferred_element_type=F32), 4)

    def sums_start(j):
        across_q = (q + 2) % DBLOCKS
        post(remote(pb.at[j, across_q, 1], rs_in.at[j, 1], rs_send.at[j, 1], rs_recv.at[j, 1], ahead_q))
        post(remote(pb.at[j, across_q, 0], rs_in.at[j, 3], rs_send.at[j, 3], rs_recv.at[j, 3], back_q))
        post(remote(pb.at[j, q_up, 0], rs_in.at[j, 0], rs_send.at[j, 0], rs_recv.at[j, 0], ahead_q))
        post(remote(pb.at[j, q_down, 1], rs_in.at[j, 2], rs_send.at[j, 2], rs_recv.at[j, 2], back_q))

    def sums_relay(j):
        arrived(rs_in.at[j, 1], rs_recv.at[j, 1])
        rl_out[j, 0] = (pf[j, q_up, 1] + rs_in[j, 1].astype(F32)).astype(BF16)
        post(remote(rl_out.at[j, 0], rs_in.at[j, 4], rs_send.at[j, 4], rs_recv.at[j, 4], ahead_q))
        arrived(rs_in.at[j, 3], rs_recv.at[j, 3])
        rl_out[j, 1] = (pf[j, q_down, 0] + rs_in[j, 3].astype(F32)).astype(BF16)
        post(remote(rl_out.at[j, 1], rs_in.at[j, 5], rs_send.at[j, 5], rs_recv.at[j, 5], back_q))

    def activate(j):
        for part, direct, relayed in ((0, 0, 5), (1, 2, 4)):
            arrived(rs_in.at[j, direct], rs_recv.at[j, direct])
            arrived(rs_in.at[j, relayed], rs_recv.at[j, relayed])
            total = pf[j, q, part] + rs_in[j, direct].astype(F32) + rs_in[j, relayed].astype(F32)
            gate_a, up_a, gate_b, up_b, expanded = [total[k] for k in range(5)]
            actb[j, q, part, 0] = (gate_a * jax.nn.sigmoid(gate_a) * up_a).astype(BF16)
            sg = jax.nn.sigmoid(gate_b)
            actb[j, q, part, 1] = (expanded * up_b * sg * (1.0 + gate_b * (1.0 - sg))).astype(BF16)
            actb[j, q, part, 2] = (expanded * gate_b * sg).astype(BF16)
        own = actb.at[j, q]
        post(remote(own, own, aq_send.at[j, 0], aq_recv.at[j, 0], ahead_q))
        post(remote(own, own, aq_send.at[j, 1], aq_recv.at[j, 1], back_q))

    def acts_relay(j):
        arrived(actb.at[j, q_down], aq_recv.at[j, 0])
        piece = actb.at[j, q_down, 0]
        post(remote(piece, piece, aq_send.at[j, 2], aq_recv.at[j, 2], ahead_q))
        arrived(actb.at[j, q_up], aq_recv.at[j, 1])
        piece = actb.at[j, q_up, 1]
        post(remote(piece, piece, aq_send.at[j, 3], aq_recv.at[j, 3], back_q))

    def second_matmul(j):
        far = (q + 2) % DBLOCKS
        arrived(actb.at[j, far, 0], aq_recv.at[j, 2])
        arrived(actb.at[j, far, 1], aq_recv.at[j, 3])
        acts = [actb[j, :, :, k].reshape(units, CHUNK) for k in range(3)]
        both = 2 * feats

        @pl.loop(0, LINE)
        def _(position):
            rows = pl.ds(pl.multiple_of(position * both, 16), both)
            ahead = jnp.dot(wt[2, rows, :], acts[0], preferred_element_type=F32)
            behind = jnp.dot(wt[0, rows, :], acts[1], preferred_element_type=F32)
            behind += jnp.dot(wt[1, rows, :], acts[2], preferred_element_type=F32)
            oacc[j, 0, rows, :] = ahead
            oacc[j, 1, rows, :] = behind
            obf[j, 0, rows, :] = ahead.astype(BF16)
            obf[j, 1, rows, :] = behind.astype(BF16)

        for position in (0, 3, 1, 2):
            post(
                remote(
                    obf.at[j, :, rows_of(position, 1 - col), :], y_in.at[j, position],
                    y_send.at[j, position], y_recv.at[j, position], across,
                )
            )

    def column_sum(j, position):
        return oacc[j, :, rows_of(position, col), :] + y_in[j, position].astype(F32)

    def scatter_line(j, t):
        for side in (0, 1):
            target = LINE - 1 - t if side == 0 else t
            sends = line < target if side == 0 else line > target
            inner = line > 0 if side == 0 else line < LINE - 1
            joins = jnp.logical_and(sends, inner)
            landing, sending = (zr_in, zr_send) if side == 0 else (zl_in, zl_send)
            if t < LINE // 2:
                arrived(y_in.at[j, target], y_recv.at[j, target])

            @pl.when(jnp.logical_and(sends, jnp.logical_not(inner)))
            def _():
                sending[j, target] = column_sum(j, target).astype(BF16)

            @pl.when(joins)
            def _():
                arrived(landing.at[j, target], z_recv.at[j, side, target])
                sending[j, target] = (column_sum(j, target) + landing[j, target].astype(F32)).astype(BF16)

            post(
                remote(
                    sending.at[j, target], landing.at[j, target], z_send.at[j, side, target],
                    z_recv.at[j, side, target], right if side == 0 else left,
                ),
                sends,
            )

    def finish(j):
        fsum[...] = column_sum(j, line)
        for side in (0, 1):
            landing = zr_in if side == 0 else zl_in

            @pl.when(line > 0 if side == 0 else line < LINE - 1)
            def _():
                arrived(landing.at[j, line], z_recv.at[j, side, line])
                fsum[...] += landing[j, line].astype(F32)

        fin[j, 0] = (fsum[0] * scale[j]).astype(BF16)
        fin[j, 1] = fsum[1].astype(BF16)
        post(remote(fin.at[j, 0], landed.at[j, 0], s_send.at[j, 0], s_recv.at[j, 0], sec_up), sec < sections - 1)
        post(remote(fin.at[j, 1], landed.at[j, 1], s_send.at[j, 1], s_recv.at[j, 1], sec_down), sec > 0)

    def deliver(j):
        for k, there in ((0, sec > 0), (1, sec < sections - 1)):

            @pl.when(there)
            def _():
                arrived(landed.at[j, k], s_recv.at[j, k])
                out_ref[k, j] = landed[j, k]

            @pl.when(jnp.logical_not(there))
            def _():
                out_ref[k, j] = jnp.zeros_like(landed[j, k])

    gather_own(0)
    gather_own(1)
    for k in range(2):
        wt[k] = gate_up[k].T
    wt[2] = down[...].T
    for t in (1, 2, 3):
        gather_step(0, t)
    gather_own(2)
    gather_rest(0)
    first_matmul(0)
    sums_start(0)
    for t in (1, 2, 3):
        gather_step(1, t)
    sums_relay(0)
    gather_rest(1)
    first_matmul(1)
    sums_start(1)
    activate(0)
    for t in (1, 2, 3):
        gather_step(2, t)
    sums_relay(1)
    acts_relay(0)
    gather_rest(2)
    first_matmul(2)
    sums_start(2)
    second_matmul(0)
    activate(1)
    sums_relay(2)
    for t in range(LINE - 1):
        scatter_line(0, t)
    acts_relay(1)
    second_matmul(1)
    activate(2)
    finish(0)
    acts_relay(2)
    for t in range(LINE - 1):
        scatter_line(1, t)
    second_matmul(2)
    finish(1)
    for t in range(LINE - 1):
        scatter_line(2, t)
    finish(2)
    for j in range(chunks):
        deliver(j)
    for copy, cond in drains:
        if cond is None:
            copy.wait_send()
        else:
            pl.when(cond)(lambda copy=copy: copy.wait_send())


def body(sections, ahead_rows, behind_rows, behind_grad, route_scores, route_counts, gate_up, down_proj):
    weights_in = gate_up[0, 0]
    weights_out = down_proj[0, 0]
    _, units, width = weights_in.shape
    slots, feats = ahead_rows.shape[1:]
    chunks = slots // CHUNK
    half = units // (2 * DBLOCKS)
    slot_ids = jnp.arange(slots, dtype=jnp.int32)
    scale_ahead = route_scores[0, 0] * (slot_ids < route_counts[0, 0]).astype(F32)
    scale_behind = route_scores[0, 1] * (slot_ids < route_counts[0, 1]).astype(F32)
    scaled_grad = (behind_grad[0].astype(F32) * scale_behind[:, None]).astype(BF16)
    rows = jnp.stack([ahead_rows[0], behind_rows[0], scaled_grad]).reshape(3, chunks, CHUNK, feats)
    xin = rows.transpose(1, 3, 0, 2).reshape(chunks, feats, 3 * CHUNK)
    vmem = pl.BlockSpec(memory_space=pltpu.VMEM)
    dma = pltpu.SemaphoreType.DMA
    piece = (5, half, CHUNK)
    out = pl.pallas_call(
        functools.partial(layer_kernel, chunks, sections),
        out_shape=jax.ShapeDtypeStruct((2, chunks, feats, CHUNK), BF16),
        in_specs=[vmem] * 4,
        out_specs=vmem,
        scratch_shapes=[
            pltpu.VMEM((chunks, width, 3 * CHUNK), BF16),
            pltpu.VMEM((3, width, units), BF16),
            pltpu.VMEM((chunks, DBLOCKS, 2) + piece, F32),
            pltpu.VMEM((chunks, DBLOCKS, 2) + piece, BF16),
            pltpu.VMEM((chunks, 6) + piece, BF16),
            pltpu.VMEM((chunks, 2) + piece, BF16),
            pltpu.VMEM((chunks, DBLOCKS, 2, 3, half, CHUNK), BF16),
            pltpu.VMEM((chunks, 2, width, CHUNK), F32),
            pltpu.VMEM((chunks, 2, width, CHUNK), BF16),
            pltpu.VMEM((chunks, LINE, 2, feats, CHUNK), BF16),
            pltpu.VMEM((chunks, LINE, 2, feats, CHUNK), BF16),
            pltpu.VMEM((chunks, LINE, 2, feats, CHUNK), BF16),
            pltpu.VMEM((chunks, LINE, 2, feats, CHUNK), BF16),
            pltpu.VMEM((chunks, LINE, 2, feats, CHUNK), BF16),
            pltpu.VMEM((chunks, 2, feats, CHUNK), BF16),
            pltpu.VMEM((chunks, 2, feats, CHUNK), BF16),
            pltpu.VMEM((2, feats, CHUNK), F32),
            dma((chunks, 20)),
            dma((chunks, 2 * LINE)),
            dma((chunks, 6)),
            dma((chunks, 6)),
            dma((chunks, 4)),
            dma((chunks, 4)),
            dma((chunks, LINE)),
            dma((chunks, LINE)),
            dma((chunks, 2, LINE)),
            dma((chunks, 2, LINE)),
            dma((chunks, 2)),
            dma((chunks, 2)),
        ],
        compiler_params=pltpu.CompilerParams(
            collective_id=0, has_side_effects=True, vmem_limit_bytes=56 * 1024 * 1024
        ),
        name="routed_layer",
    )(xin, weights_in, weights_out, scale_ahead.reshape(chunks, 1, CHUNK))
    moved = out.transpose(0, 1, 3, 2).reshape(2, slots, feats)
    return (moved[0][None], moved[1][None])


def solution(mesh):
    in_specs = (
        P("section", None, "expert"),
        P("section", None, "expert"),
        P("section", None, "expert"),
        P("section", None, None),
        P("section", None),
        P("section", "expert", None, None, None),
        P("section", "expert", None, None),
    )
    out_specs = (P("section", None, "expert"), P("section", None, "expert"))
    step = functools.partial(body, mesh.shape["section"])
    return jax.shard_map(step, mesh=mesh, in_specs=in_specs, out_specs=out_specs, check_vma=False)
```

time: 468 us -> 173 us (0.37)
  the two profiles are of different devices: /device:TPU:88 before, /device:TPU:5 now
where the time goes in v1:
time: 173 us
  Pallas kernels  161 us (93%)
  local copies, waits for them, and re-layouts  8.26 us (5%)
  other arithmetic  2.95 us (2%)
    pallas_call x1, Pallas kernels, body(): pl.pallas_call(functools.partial(layer_kernel, chunks, sections), out_sha...  161 us
    unnamed x6, local copies, waits for them, and re-layouts  3.72 us

profile of v1, /device:TPU:5, one launch (start us, length us, event | category | flops | bytes accessed | tf_op | source)
XLA Modules:
  0.0 173.1 jit_solution(5507074238117804275)
XLA Ops:
  0.6 1.3 fusion.2
  1.9 0.7 slice_reduce_fusion
  2.6 0.6 fusion
  3.3 1.0 multiply_convert_fusion
  4.3 0.1 copy.14
  4.4 1.1 copy.12
  5.5 0.0 copy-start
  5.5 1.1 copy.13
  6.5 0.1 maximum_bitcast_fusion
  6.7 1.0 copy.16.xin
  7.8 0.0 copy-done
  7.8 1.2 compare_select_fusion.scale
  9.0 161.2 %routed_layer.1 = bf16[2,3,224,128]{3,2,1,0:T(8,128)(2,1)} custom-call(bf16[3,224,384]{2,1,0:T(8,128)(2,1)} %copy.16.xin, bf16[2,256,1792]{2,1,0:T(8,128)(2,1)} %bitcast.16, bf16[256,1792]{1,0:T(8,128)(2,1)} %bitcast.18, f32[3,1,128]{2,1,0:T(1,128)} %compare_select_fusion.scale), custom_call_target="tpu_custom_call" | custom-call | tf_op jit(solution)/shard_map/routed_layer/pallas_call | solution.py:297
  170.2 1.0 fusion.1
  171.2 0.1 copy.17
  171.4 0.8 copy.19
  172.2 0.1 copy.18
  172.3 0.8 copy.20
  (1 shorter events, 0.0 us)
Async XLA Ops:
  5.5 2.3 %copy-start = (f32[1,2,384]{2,1,0:T(2,128)S(1)}, f32[1,2,384]{2,1,0:T(2,128)}, u32[]{:S(2)}) copy-start(f32[1,2,384]{2,1,0:T(2,128)} %param.10) | copy-start | bytes 9220

commit v2 on v1

--- a/solution.py
+++ b/solution.py
@@ -16,11 +16,11 @@
 
 
 def layer_kernel(
-    chunks, sections, xin, gate_up, down, scale, out_ref,
-    xall, wt, pf, pb, rs_in, rl_out, actb, oacc, obf, y_in, zl_send, zr_send, zl_in, zr_in, fin, landed, fsum,
-    ag_send, ag_recv, rs_send, rs_recv, aq_send, aq_recv, y_send, y_recv, z_send, z_recv, s_send, s_recv,
+    chunks, sections, ahead, behind, grad, scores, counts, gate_up, down, out_ahead, out_behind,
+    w, xall, wt, pf, pb, rs_in, rl_out, actb, oacc, obf, y_in, zl_send, zr_send, zl_in, zr_in, fin, landed, fsum,
+    w_sem, ag_send, ag_recv, rs_send, rs_recv, aq_send, aq_recv, y_send, y_recv, z_send, z_recv, s_send, s_recv,
 ):
-    feats = xin.shape[1]
+    feats = ahead.shape[0]
     units = down.shape[0]
     half = units // (2 * DBLOCKS)
     me = lax.axis_index("expert")
@@ -41,10 +41,13 @@
     sec_up = {"section": (sec + 1) % sections}
     sec_down = {"section": (sec + sections - 1) % sections}
 
+    loads = [pltpu.make_async_copy(gate_up.at[k], w.at[k], w_sem.at[k]) for k in range(2)]
+    loads.append(pltpu.make_async_copy(down, w.at[2], w_sem.at[2]))
+    for load in loads:
+        load.start()
     barrier = pltpu.get_barrier_semaphore()
     for peer in (right, left, across, ahead_q, back_q, sec_up, sec_down):
         pl.semaphore_signal(barrier, inc=1, device_id=peer, device_id_type=MESH)
-    pl.semaphore_wait(barrier, 7)
 
     drains = []
 
@@ -69,13 +72,23 @@
     def slot_of(position, column):
         return position * 2 + column
 
+    def scale_of(m, j):
+        slots = lax.broadcasted_iota(jnp.int32, (1, CHUNK), 1) + j * CHUNK
+        return jnp.where(slots < counts[m], scores[m : m + 1, j * CHUNK : (j + 1) * CHUNK], 0.0)
+
+    def place_own(j):
+        slots = slice(j * CHUNK, (j + 1) * CHUNK)
+        mine = rows_of(line, col)
+        xall[j, mine, :CHUNK] = ahead[:, slots]
+        xall[j, mine, CHUNK : 2 * CHUNK] = behind[:, slots]
+        xall[j, mine, 2 * CHUNK :] = (grad[:, slots].astype(F32) * scale_of(1, j)).astype(BF16)
+
     def gather_own(j):
         spot = xall.at[j, rows_of(line, col), :]
         sem = ag_recv.at[j, slot_of(line, col)]
-        post(remote(xin.at[j], spot, ag_send.at[j, 0], sem, right), line < LINE - 1)
-        post(remote(xin.at[j], spot, ag_send.at[j, 1], sem, left), line > 0)
-        post(remote(xin.at[j], spot, ag_send.at[j, 2], sem, across))
-        xall[j, rows_of(line, col), :] = xin[j]
+        post(remote(spot, spot, ag_send.at[j, 0], sem, right), line < LINE - 1)
+        post(remote(spot, spot, ag_send.at[j, 1], sem, left), line > 0)
+        post(remote(spot, spot, ag_send.at[j, 2], sem, across))
 
     def gather_step(j, t):
         for side in (0, 1):
@@ -89,6 +102,15 @@
                 post(remote(spot, spot, ag_send.at[j, 3 * t + side], sem, right if side == 0 else left), onward)
             post(remote(spot, spot, ag_send.at[j, 12 + 2 * t + side], sem, across), there)
 
+    def gather_step1(j):
+        gather_step(j, 1)
+
+    def gather_step2(j):
+        gather_step(j, 2)
+
+    def gather_step3(j):
+        gather_step(j, 3)
+
     def gather_rest(j):
         for position in range(LINE):
             arrived(xall.at[j, rows_of(position, 1 - col), :], ag_recv.at[j, slot_of(position, 1 - col)])
@@ -102,10 +124,10 @@
                     pb[j, block, part, comp] = rows.astype(BF16)
 
         for k in range(2):
-            value = jnp.dot(gate_up[k], xall[j, :, : 2 * CHUNK], preferred_element_type=F32)
+            value = jnp.dot(w[k], xall[j, :, : 2 * CHUNK], preferred_element_type=F32)
             keep(value[:, :CHUNK], k)
             keep(value[:, CHUNK:], 2 + k)
-        keep(jnp.dot(down[...], xall[j, :, 2 * CHUNK :], preferred_element_type=F32), 4)
+        keep(jnp.dot(w[2], xall[j, :, 2 * CHUNK :], preferred_element_type=F32), 4)
 
     def sums_start(j):
         across_q = (q + 2) % DBLOCKS
@@ -173,7 +195,11 @@
     def column_sum(j, position):
         return oacc[j, :, rows_of(position, col), :] + y_in[j, position].astype(F32)
 
-    def scatter_line(j, t):
+    def scatter_line(j):
+        for t in range(LINE - 1):
+            scatter_target(j, t)
+
+    def scatter_target(j, t):
         for side in (0, 1):
             target = LINE - 1 - t if side == 0 else t
             sends = line < target if side == 0 else line > target
@@ -210,67 +236,47 @@
                 arrived(landing.at[j, line], z_recv.at[j, side, line])
                 fsum[...] += landing[j, line].astype(F32)
 
-        fin[j, 0] = (fsum[0] * scale[j]).astype(BF16)
+        fin[j, 0] = (fsum[0] * scale_of(0, j)).astype(BF16)
         fin[j, 1] = fsum[1].astype(BF16)
         post(remote(fin.at[j, 0], landed.at[j, 0], s_send.at[j, 0], s_recv.at[j, 0], sec_up), sec < sections - 1)
         post(remote(fin.at[j, 1], landed.at[j, 1], s_send.at[j, 1], s_recv.at[j, 1], sec_down), sec > 0)
 
     def deliver(j):
-        for k, there in ((0, sec > 0), (1, sec < sections - 1)):
+        slots = slice(j * CHUNK, (j + 1) * CHUNK)
+        for k, there, out in ((0, sec > 0, out_ahead), (1, sec < sections - 1, out_behind)):
 
             @pl.when(there)
             def _():
                 arrived(landed.at[j, k], s_recv.at[j, k])
-                out_ref[k, j] = landed[j, k]
+                out[:, slots] = landed[j, k]
 
             @pl.when(jnp.logical_not(there))
             def _():
-                out_ref[k, j] = jnp.zeros_like(landed[j, k])
-
-    gather_own(0)
+                out[:, slots] = jnp.zeros((feats, CHUNK), BF16)
+
+    def enter(j):
+        gather_rest(j)
+        first_matmul(j)
+        sums_start(j)
+
+    place_own(1)
+    pl.semaphore_wait(barrier, 7)
     gather_own(1)
-    for k in range(2):
-        wt[k] = gate_up[k].T
-    wt[2] = down[...].T
-    for t in (1, 2, 3):
-        gather_step(0, t)
+    place_own(2)
     gather_own(2)
-    gather_rest(0)
-    first_matmul(0)
-    sums_start(0)
-    for t in (1, 2, 3):
-        gather_step(1, t)
-    sums_relay(0)
-    gather_rest(1)
-    first_matmul(1)
-    sums_start(1)
-    activate(0)
-    for t in (1, 2, 3):
-        gather_step(2, t)
-    sums_relay(1)
-    acts_relay(0)
-    gather_rest(2)
-    first_matmul(2)
-    sums_start(2)
-    second_matmul(0)
-    activate(1)
-    sums_relay(2)
-    for t in range(LINE - 1):
-        scatter_line(0, t)
-    acts_relay(1)
-    second_matmul(1)
-    activate(2)
-    finish(0)
-    acts_relay(2)
-    for t in range(LINE - 1):
-        scatter_line(1, t)
-    second_matmul(2)
-    finish(1)
-    for t in range(LINE - 1):
-        scatter_line(2, t)
-    finish(2)
-    for j in range(chunks):
-        deliver(j)
+    place_own(0)
+    for k in range(3):
+        loads[k].wait()
+        wt[k] = w[k].T
+    for step, j in (
+        (gather_step1, 1), (gather_own, 0), (gather_step2, 1), (gather_step3, 1), (gather_step1, 0),
+        (gather_step2, 0), (gather_step1, 2), (gather_step3, 0), (enter, 1), (gather_step2, 2), (enter, 0),
+        (sums_relay, 1), (sums_relay, 0), (activate, 1), (gather_step3, 2), (enter, 2), (activate, 0),
+        (sums_relay, 2), (acts_relay, 0), (activate, 2), (acts_relay, 1), (second_matmul, 0), (acts_relay, 2),
+        (second_matmul, 1), (scatter_line, 0), (second_matmul, 2), (scatter_line, 1), (finish, 0),
+        (scatter_line, 2), (finish, 1), (finish, 2), (deliver, 1), (deliver, 0), (deliver, 2),
+    ):
+        step(j)
     for copy, cond in drains:
         if cond is None:
             copy.wait_send()
@@ -285,21 +291,19 @@
     slots, feats = ahead_rows.shape[1:]
     chunks = slots // CHUNK
     half = units // (2 * DBLOCKS)
-    slot_ids = jnp.arange(slots, dtype=jnp.int32)
-    scale_ahead = route_scores[0, 0] * (slot_ids < route_counts[0, 0]).astype(F32)
-    scale_behind = route_scores[0, 1] * (slot_ids < route_counts[0, 1]).astype(F32)
-    scaled_grad = (behind_grad[0].astype(F32) * scale_behind[:, None]).astype(BF16)
-    rows = jnp.stack([ahead_rows[0], behind_rows[0], scaled_grad]).reshape(3, chunks, CHUNK, feats)
-    xin = rows.transpose(1, 3, 0, 2).reshape(chunks, feats, 3 * CHUNK)
     vmem = pl.BlockSpec(memory_space=pltpu.VMEM)
+    smem = pl.BlockSpec(memory_space=pltpu.SMEM)
+    here = pl.BlockSpec(memory_space=pl.ANY)
     dma = pltpu.SemaphoreType.DMA
+    out = jax.ShapeDtypeStruct((feats, slots), BF16)
     piece = (5, half, CHUNK)
-    out = pl.pallas_call(
+    moved = pl.pallas_call(
         functools.partial(layer_kernel, chunks, sections),
-        out_shape=jax.ShapeDtypeStruct((2, chunks, feats, CHUNK), BF16),
-        in_specs=[vmem] * 4,
-        out_specs=vmem,
+        out_shape=(out, out),
+        in_specs=[vmem, vmem, vmem, vmem, smem, here, here],
+        out_specs=(vmem, vmem),
         scratch_shapes=[
+            pltpu.VMEM((3, units, width), BF16),
             pltpu.VMEM((chunks, width, 3 * CHUNK), BF16),
             pltpu.VMEM((3, width, units), BF16),
             pltpu.VMEM((chunks, DBLOCKS, 2) + piece, F32),
@@ -317,6 +321,7 @@
             pltpu.VMEM((chunks, 2, feats, CHUNK), BF16),
             pltpu.VMEM((chunks, 2, feats, CHUNK), BF16),
             pltpu.VMEM((2, feats, CHUNK), F32),
+            dma((3,)),
             dma((chunks, 20)),
             dma((chunks, 2 * LINE)),
             dma((chunks, 6)),
@@ -334,9 +339,10 @@
             collective_id=0, has_side_effects=True, vmem_limit_bytes=56 * 1024 * 1024
         ),
         name="routed_layer",
-    )(xin, weights_in, weights_out, scale_ahead.reshape(chunks, 1, CHUNK))
-    moved = out.transpose(0, 1, 3, 2).reshape(2, slots, feats)
-    return (moved[0][None], moved[1][None])
+    )(
+        ahead_rows[0].T, behind_rows[0].T, behind_grad[0].T, route_scores[0], route_counts[0], weights_in, weights_out
+    )
+    return (moved[0].T[None], moved[1].T[None])
 
 
 def solution(mesh):

time: 173 us -> 156 us (0.902)
  the two profiles are of different devices: /device:TPU:5 before, /device:TPU:13 now
where the time goes in v2:
time: 156 us
  Pallas kernels  152 us (97%)
  local copies, waits for them, and re-layouts  3.21 us (2%)
    pallas_call x1, Pallas kernels, body(): pl.pallas_call(functools.partial(layer_kernel, chunks, sections), out_sha...  152 us
    unnamed x2, local copies, waits for them, and re-layouts  3.21 us

profile of v2, /device:TPU:13, one launch (start us, length us, event | category | flops | bytes accessed | tf_op | source)
XLA Modules:
  0.0 156.1 jit_solution(5132951970109333982)
XLA Ops:
  0.6 152.3 %routed_layer.1 = (bf16[224,384]{1,0:T(8,128)(2,1)}, bf16[224,384]{1,0:T(8,128)(2,1)}) custom-call(bf16[224,384]{1,0:T(8,128)(2,1)} %bitcast.23, bf16[224,384]{1,0:T(8,128)(2,1)} %bitcast.24, bf16[224,384]{1,0:T(8,128)(2,1)} %bitcast.25, f32[2,384]{1,0:T(2,128)} %bitcast.26, s32[2]{0:T(128)} %bitcast.27, bf16[2,256,1792]{2,1,0:T(8,128)(2,1)} %bitcast.19, ...), custom_call_target="tpu_custom_call" | custom-call | tf_op jit(solution)/shard_map/routed_layer/pallas_call | solution.py:300
  152.9 1.6 %copy.11 = bf16[1,384,224]{1,2,0:T(8,128)(2,1)} copy(bf16[1,384,224]{1,2,0:T(8,128)(2,1)} %bitcast.22) | data formatting | bytes 344064
  154.5 1.6 %copy.12 = bf16[1,384,224]{1,2,0:T(8,128)(2,1)} copy(bf16[1,384,224]{1,2,0:T(8,128)(2,1)} %bitcast.21) | data formatting | bytes 344064

commit v3 on v2

--- a/solution.py
+++ b/solution.py
@@ -121,7 +121,6 @@
                 for part in range(2):
                     rows = value[(2 * block + part) * half : (2 * block + part + 1) * half]
                     pf[j, block, part, comp] = rows
-                    pb[j, block, part, comp] = rows.astype(BF16)
 
         for k in range(2):
             value = jnp.dot(w[k], xall[j, :, : 2 * CHUNK], preferred_element_type=F32)
@@ -130,24 +129,23 @@
         keep(jnp.dot(w[2], xall[j, :, 2 * CHUNK :], preferred_element_type=F32), 4)
 
     def sums_start(j):
-        across_q = (q + 2) % DBLOCKS
-        post(remote(pb.at[j, across_q, 1], rs_in.at[j, 1], rs_send.at[j, 1], rs_recv.at[j, 1], ahead_q))
-        post(remote(pb.at[j, across_q, 0], rs_in.at[j, 3], rs_send.at[j, 3], rs_recv.at[j, 3], back_q))
-        post(remote(pb.at[j, q_up, 0], rs_in.at[j, 0], rs_send.at[j, 0], rs_recv.at[j, 0], ahead_q))
-        post(remote(pb.at[j, q_down, 1], rs_in.at[j, 2], rs_send.at[j, 2], rs_recv.at[j, 2], back_q))
+        far = (q + 2) % DBLOCKS
+        for slot, block, part in ((0, q_up, 0), (1, far, 1), (2, far, 0), (3, q_down, 1)):
+            pb[j, slot] = pf[j, block, part].astype(BF16)
+        for way, device in ((0, ahead_q), (1, back_q)):
+            pair = pl.ds(2 * way, 2)
+            post(remote(pb.at[j, pair], rs_in.at[j, pair], rs_send.at[j, way], rs_recv.at[j, way], device))
 
     def sums_relay(j):
-        arrived(rs_in.at[j, 1], rs_recv.at[j, 1])
-        rl_out[j, 0] = (pf[j, q_up, 1] + rs_in[j, 1].astype(F32)).astype(BF16)
-        post(remote(rl_out.at[j, 0], rs_in.at[j, 4], rs_send.at[j, 4], rs_recv.at[j, 4], ahead_q))
-        arrived(rs_in.at[j, 3], rs_recv.at[j, 3])
-        rl_out[j, 1] = (pf[j, q_down, 0] + rs_in[j, 3].astype(F32)).astype(BF16)
-        post(remote(rl_out.at[j, 1], rs_in.at[j, 5], rs_send.at[j, 5], rs_recv.at[j, 5], back_q))
+        for way, slot, block, part, device in ((0, 1, q_up, 1, ahead_q), (1, 2, q_down, 0, back_q)):
+            arrived(rs_in.at[j, pl.ds(2 * way, 2)], rs_recv.at[j, way])
+            rl_out[j, way] = (pf[j, block, part] + rs_in[j, slot].astype(F32)).astype(BF16)
+            sems = rs_send.at[j, 2 + way], rs_recv.at[j, 2 + way]
+            post(remote(rl_out.at[j, way], rs_in.at[j, 4 + way], *sems, device))
 
     def activate(j):
-        for part, direct, relayed in ((0, 0, 5), (1, 2, 4)):
-            arrived(rs_in.at[j, direct], rs_recv.at[j, direct])
-            arrived(rs_in.at[j, relayed], rs_recv.at[j, relayed])
+        for part, direct, relayed in ((0, 0, 5), (1, 3, 4)):
+            arrived(rs_in.at[j, relayed], rs_recv.at[j, relayed - 2])
             total = pf[j, q, part] + rs_in[j, direct].astype(F32) + rs_in[j, relayed].astype(F32)
             gate_a, up_a, gate_b, up_b, expanded = [total[k] for k in range(5)]
             actb[j, q, part, 0] = (gate_a * jax.nn.sigmoid(gate_a) * up_a).astype(BF16)
@@ -259,22 +257,22 @@
         first_matmul(j)
         sums_start(j)
 
+    place_own(0)
+    pl.semaphore_wait(barrier, 7)
+    gather_own(0)
     place_own(1)
-    pl.semaphore_wait(barrier, 7)
     gather_own(1)
     place_own(2)
-    gather_own(2)
-    place_own(0)
     for k in range(3):
         loads[k].wait()
         wt[k] = w[k].T
     for step, j in (
-        (gather_step1, 1), (gather_own, 0), (gather_step2, 1), (gather_step3, 1), (gather_step1, 0),
-        (gather_step2, 0), (gather_step1, 2), (gather_step3, 0), (enter, 1), (gather_step2, 2), (enter, 0),
-        (sums_relay, 1), (sums_relay, 0), (activate, 1), (gather_step3, 2), (enter, 2), (activate, 0),
-        (sums_relay, 2), (acts_relay, 0), (activate, 2), (acts_relay, 1), (second_matmul, 0), (acts_relay, 2),
-        (second_matmul, 1), (scatter_line, 0), (second_matmul, 2), (scatter_line, 1), (finish, 0),
-        (scatter_line, 2), (finish, 1), (finish, 2), (deliver, 1), (deliver, 0), (deliver, 2),
+        (gather_step1, 0), (gather_own, 2), (gather_step2, 0), (gather_step1, 1), (gather_step3, 0),
+        (gather_step2, 1), (gather_step3, 1), (enter, 0), (gather_step1, 2), (gather_step2, 2), (enter, 1),
+        (sums_relay, 0), (gather_step3, 2), (enter, 2), (sums_relay, 1), (activate, 0), (activate, 1),
+        (acts_relay, 0), (sums_relay, 2), (acts_relay, 1), (second_matmul, 0), (activate, 2),
+        (second_matmul, 1), (acts_relay, 2), (scatter_line, 0), (second_matmul, 2), (scatter_line, 1),
+        (finish, 0), (scatter_line, 2), (finish, 1), (finish, 2), (deliver, 0), (deliver, 1), (deliver, 2),
     ):
         step(j)
     for copy, cond in drains:
@@ -307,7 +305,7 @@
             pltpu.VMEM((chunks, width, 3 * CHUNK), BF16),
             pltpu.VMEM((3, width, units), BF16),
             pltpu.VMEM((chunks, DBLOCKS, 2) + piece, F32),
-            pltpu.VMEM((chunks, DBLOCKS, 2) + piece, BF16),
+            pltpu.VMEM((chunks, 4) + piece, BF16),
             pltpu.VMEM((chunks, 6) + piece, BF16),
             pltpu.VMEM((chunks, 2) + piece, BF16),
             pltpu.VMEM((chunks, DBLOCKS, 2, 3, half, CHUNK), BF16),
@@ -324,8 +322,8 @@
             dma((3,)),
             dma((chunks, 20)),
             dma((chunks, 2 * LINE)),
-            dma((chunks, 6)),
-            dma((chunks, 6)),
+            dma((chunks, 4)),
+            dma((chunks, 4)),
             dma((chunks, 4)),
             dma((chunks, 4)),
             dma((chunks, LINE)),
@@ -342,7 +340,10 @@
     )(
         ahead_rows[0].T, behind_rows[0].T, behind_grad[0].T, route_scores[0], route_counts[0], weights_in, weights_out
     )
-    return (moved[0].T[None], moved[1].T[None])
+    sec = lax.axis_index("section")
+    got_ahead = jnp.where(sec > 0, moved[0], jnp.zeros_like(moved[0]))
+    got_behind = jnp.where(sec < sections - 1, moved[1], jnp.zeros_like(moved[1]))
+    return (got_ahead.T[None], got_behind.T[None])
 
 
 def solution(mesh):

time: 156 us -> 153 us (0.981)
  local copies, waits for them, and re-layouts: 3.21 us -> 0 us
  Pallas kernels: 152 us -> 150 us
  other arithmetic: 0 us -> 1.78 us
    unnamed x2 -> x0, local copies, waits for them, and re-layouts: 3.21 us -> none
    pallas_call x1, Pallas kernels: 152 us -> 150 us  [body(): pl.pallas_call(functools.partial(layer_kernel, chunks, sections), out_sha...]
    broadcast_in_dim x0 -> x1, other arithmetic: none -> 1.78 us  [body(): return (got_ahead.T[None], got_behind.T[None])]
where the time goes in v3:
time: 153 us
  Pallas kernels  150 us (98%)
  other arithmetic  1.78 us (1%)
    pallas_call x1, Pallas kernels, body(): pl.pallas_call(functools.partial(layer_kernel, chunks, sections), out_sha...  150 us

profile of v3, /device:TPU:13, one launch (start us, length us, event | category | flops | bytes accessed | tf_op | source)
XLA Modules:
  0.0 152.9 jit_solution(16659632673606360939)
XLA Ops:
  0.6 150.5 %routed_layer.1 = (bf16[224,384]{1,0:T(8,128)(2,1)}, bf16[224,384]{1,0:T(8,128)(2,1)}) custom-call(bf16[224,384]{1,0:T(8,128)(2,1)} %bitcast.23, bf16[224,384]{1,0:T(8,128)(2,1)} %bitcast.24, bf16[224,384]{1,0:T(8,128)(2,1)} %bitcast.25, f32[2,384]{1,0:T(2,128)} %bitcast.26, s32[2]{0:T(128)} %bitcast.27, bf16[2,256,1792]{2,1,0:T(8,128)(2,1)} %bitcast.21, ...), custom_call_target="tpu_custom_call" | custom-call | tf_op jit(solution)/shard_map/routed_layer/pallas_call | solution.py:298
  151.1 1.8 %select_bitcast_fusion = (bf16[1,384,224]{1,2,0:T(8,128)(2,1)}, bf16[1,384,224]{1,2,0:T(8,128)(2,1)}) fusion(bf16[224,384]{1,0:T(8,128)(2,1)} %get-tuple-element.5, pred[]{:T(512)S(6)} %lt.3, bf16[224,384]{1,0:T(8,128)(2,1)} %get-tuple-element.4, pred[]{:T(512)S(6)} %gt.3), kind=kLoop, calls=%fused_computation | loop fusion | flops 172032 | bytes 688130 | tf_op jit(solution)/shard_map/broadcast_in_dim | solution.py:346
